TPU v7x, 256 devices: a whole 4x4x8 slice. The times are simulated.
256 devices in a mesh: gx: 16 (over y_lo, x, core), gy: 16 (over y_hi, z).
Axes of the slice: x: 4, y: 4 (y_hi: 2, y_lo: 2; y = y_hi * 2 + y_lo), z: 8, core: 2. Of those that a mesh axis runs over, the one named last changes fastest.
Arguments:
- operator: bfloat16 [16, 16, 2, 1536, 1536], P('gx', 'gy'), may hold values from -0.0390625 to 0.0390625
- incident: bfloat16 [16, 16, 2, 1536, 128], P('gx', 'gy'), may hold values from -6 to 6
- feed: bfloat16 [16, 16, 2, 1536], P('gx', 'gy'), may hold values from -24 to 24
- port_element: int32 [128], replicated, may hold values from 0 to 255
- positions: int32 [16, 16, 2], P('gx', 'gy'), may hold values from 0 to 122, as said below
Outputs:
- currents: bfloat16 [16, 16, 2, 1536, 128], P('gx', 'gy')
- fields: float32 [2048, 2, 128], P(('gx', 'gy'))
Inputs may be any that keep to these rules, and one draw needn't show every extreme that they name: `positions`: element (c, r) lies at (c * 8 + j0, r * 8 + j1) with 0 <= j0, j1 < 3.
All inputs are finite; a program needn't handle non-finite values.
Results may differ from a plain program's by a relative error of at most 0.008.
Values may be sent and summed in bfloat16 or wider, within the bound.
No kernel may reach another device: no remote copies, remote signals or barrier semaphores. Data moves between devices by JAX's collectives and lax.ppermute only.
A program may use at most 64 MiB of HBM per device.

v0:
```python
import functools
import math

import jax
import jax.numpy as jnp
import ml_dtypes
import numpy as np
from jax import lax
from jax.experimental import pallas as pl
from jax.experimental.pallas import tpu as pltpu
from jax.sharding import PartitionSpec as P

THETAS = 32
PHIS = 64
ITERS = 3
SPACING = 8
WAVE = 2
FACE = 384
PORTS = 128
ORDER = 4 * FACE
WIDE = 2 * PORTS
ANGLES = THETAS * PHIS
HALF_PHIS = PHIS // 2
STEP_THETAS = 4
STEPS = THETAS // 2 // STEP_THETAS
STEP_ROWS = STEP_THETAS * HALF_PHIS
STEP_DIRS = STEP_THETAS * PHIS


VMEM = pltpu.VMEM
HBM = pltpu.HBM
VMEM_LIMIT = 16 << 20
UNROLL = 4
F32 = jnp.float32
BF16 = jnp.bfloat16


def theta_order():
    owner = np.arange(THETAS) // 2
    return [np.nonzero(owner % 2 == parity)[0] for parity in (0, 1)]


def face_tables():
    along = (np.arange(FACE) + 0.5) * (SPACING / FACE)
    sin_theta = np.sin((np.arange(THETAS) + 0.5) * (math.pi / (2.0 * THETAS)))
    sin_phi = np.sin(np.arange(HALF_PHIS) * (2.0 * math.pi / PHIS))
    angle = (2.0 * math.pi / WAVE) * (sin_theta[:, None] * sin_phi[None, :])[:, :, None] * along
    blocks = []
    for order in theta_order():
        for step in range(STEPS):
            part = angle[order[step * STEP_THETAS : (step + 1) * STEP_THETAS]]
            part = part.reshape(STEP_ROWS, FACE)
            blocks.append(np.concatenate([np.cos(part), np.sin(part)], axis=0))
    return np.stack(blocks).astype(ml_dtypes.bfloat16)


def direction_cosines():
    order = np.concatenate(theta_order())
    theta = (order + 0.5) * (math.pi / (2.0 * THETAS))
    azimuth = np.arange(PHIS) * (2.0 * math.pi / PHIS)
    dir_x = np.sin(theta)[:, None] * np.cos(azimuth)[None, :]
    dir_y = np.sin(theta)[:, None] * np.sin(azimuth)[None, :]
    whole = np.stack([dir_x.reshape(2 * STEPS, STEP_DIRS), dir_y.reshape(2 * STEPS, STEP_DIRS)], axis=1)
    return whole.astype(np.float32)


def swapped(vec):
    return jnp.concatenate([-vec[:, PORTS:], vec[:, :PORTS]], axis=1)


def faces_in_order():
    odd_x = lax.rem(lax.axis_index("gx"), 2)
    odd_y = lax.rem(lax.axis_index("gy"), 2)
    return (2 + odd_y, 3 - odd_y, odd_x, 1 - odd_x)


def face_rows(face):
    return pl.ds(pl.multiple_of(face * FACE, FACE), FACE)


def slot_product(oper_ref, slot, cols, vec, vec_swapped):
    return jnp.dot(oper_ref[slot, 0, :, cols], vec, preferred_element_type=F32) + jnp.dot(
        oper_ref[slot, 1, :, cols], vec_swapped, preferred_element_type=F32
    )


ALL_COLS = slice(0, ORDER)
NEAR_COLS = slice(0, 2 * FACE)
FAR_COLS = slice(2 * FACE, ORDER)


def base_first_kernel(oper_hbm, incident_hbm, feed_hbm, ports_hbm, oper_ref, rhs_ref, base_ref, *rest):
    outs, (incident, feed, ports, natural_ref, sems, small_sems) = rest[:2], rest[2:]
    faces = faces_in_order()
    columns = columns_in_order(faces)
    small = [
        pltpu.make_async_copy(source, target, small_sems.at[index])
        for index, (source, target) in enumerate(((incident_hbm, incident), (feed_hbm, feed), (ports_hbm, ports)))
    ]
    large = [operator_copies(oper_hbm, oper_ref, slot, face, columns, sems) for slot, face in enumerate(faces)]
    for copy in small + large[0] + large[1]:
        copy.start()
    for copy in small:
        copy.wait()
    myself = lax.axis_index("gx") * lax.axis_size("gy") + lax.axis_index("gy")
    selected = (ports[...] == myself).astype(F32).astype(BF16)
    blank = jnp.zeros_like(selected)
    select = jnp.concatenate(
        [jnp.concatenate([selected, blank], axis=1), jnp.concatenate([blank, selected], axis=1)], axis=0
    )
    fed = lax.dot_general(feed[...], select, (((0,), (0,)), ((), ())), preferred_element_type=F32)
    both = jnp.concatenate([incident[0], incident[1]], axis=1)
    natural_ref[...] = (both.astype(F32) + fed).astype(BF16)
    for index, face in enumerate(columns):
        rhs_ref[pl.ds(index * FACE, FACE), :] = natural_ref[face_rows(face), :]
    rhs = rhs_ref[...]
    rhs_swapped = swapped(rhs)
    for slot in range(2):
        for copy in large[slot]:
            copy.wait()
        for copy in large[slot + 2]:
            copy.start()
        base_slot(oper_ref, rhs, rhs_swapped, slot, base_ref, outs)
    for copy in large[2] + large[3]:
        copy.wait()


def columns_in_order(faces):
    return (faces[1], faces[3], faces[0], faces[2])


def column_of(slot):
    return (2, 0, 3, 1)[slot]


def operator_copies(oper_hbm, oper_ref, slot, face, columns, sems):
    return [
        pltpu.make_async_copy(
            oper_hbm.at[:, face_rows(face), face_rows(column)],
            oper_ref.at[slot, :, :, pl.ds(index * FACE, FACE)],
            sems.at[slot, index],
        )
        for index, column in enumerate(columns)
    ]


def base_slot(oper_ref, rhs, rhs_swapped, slot, base_ref, outs):
    start = column_of(slot) * FACE
    own = rhs[start : start + FACE].astype(F32)
    base = 0.5 * own + slot_product(oper_ref, slot, ALL_COLS, rhs, rhs_swapped)
    at = slot % len(outs)
    base_ref[at] = base
    outs[at][...] = (2.0 * base).astype(BF16)


def base_second_kernel(slot, oper_ref, rhs_ref, base_ref, out_ref):
    rhs = rhs_ref[...]
    base_slot(oper_ref, rhs, swapped(rhs), slot, base_ref, (out_ref,))


def joined(first_ref, second_ref):
    trace = jnp.concatenate([first_ref[...], second_ref[...]], axis=0)
    return trace, swapped(trace)


def near_kernel(oper_ref, base_first_ref, base_second_ref, base_third_ref, near_y_ref, near_x_ref, *outs):
    trace, trace_swapped = joined(near_y_ref, near_x_ref)
    for slot in range(4):
        base = (base_first_ref, base_first_ref, base_second_ref, base_third_ref)[slot][slot % 2 if slot < 2 else 0]
        outs[slot // 2][slot % 2] = base + slot_product(oper_ref, slot, NEAR_COLS, trace, trace_swapped)


def step_slots(oper_ref, part_ref, trace, trace_swapped, first, outs):
    for index in range(2):
        coupled = slot_product(oper_ref, first + index, FAR_COLS, trace, trace_swapped)
        outs[index][...] = (2.0 * (part_ref[index] + coupled)).astype(BF16)


def step_first_kernel(oper_ref, part_ref, far_y_ref, far_x_ref, first_ref, second_ref, trace_ref):
    trace, trace_swapped = joined(far_y_ref, far_x_ref)
    trace_ref[...] = trace
    step_slots(oper_ref, part_ref, trace, trace_swapped, 0, (first_ref, second_ref))


def step_second_kernel(slot, oper_ref, part_ref, trace_ref, out_ref):
    trace = trace_ref[...]
    coupled = slot_product(oper_ref, slot, FAR_COLS, trace, swapped(trace))
    out_ref[...] = (2.0 * (part_ref[slot - 2] + coupled)).astype(BF16)


def last_kernel(oper_ref, part_first_ref, part_second_ref, *rest):
    traces, tables_ref, phases_ref = rest[:4], rest[4], rest[5]
    currents_hbm, vec_ref, out_ref, split_ref, sem = rest[6:]
    trace, trace_swapped = joined(traces[0], traces[2])
    for slot, face in enumerate(faces_in_order()):
        rows = face_rows(face)
        part = (part_first_ref if slot < 2 else part_second_ref)[slot % 2]
        coupled = slot_product(oper_ref, slot, FAR_COLS, trace, trace_swapped)
        currents = (part + 0.5 * traces[slot][...].astype(F32) + coupled).astype(BF16)
        vec_ref[rows, :] = currents
        split_ref[0, rows, :] = currents[:, :PORTS]
        split_ref[1, rows, :] = currents[:, PORTS:]
    copy = pltpu.make_async_copy(split_ref, currents_hbm, sem)
    copy.start()
    field_steps(1 - lax.rem(lax.axis_index("gx"), 2), tables_ref, phases_ref, vec_ref, out_ref)
    copy.wait()


def own_field_kernel(tables_ref, phases_ref, vec_ref, out_ref):
    field_steps(lax.rem(lax.axis_index("gx"), 2), tables_ref, phases_ref, vec_ref, out_ref)


def field_steps(parity, tables_ref, phases_ref, vec_ref, out_ref):
    def body(step, carry):
        field_step(parity * STEPS + step, step, tables_ref, phases_ref, vec_ref, out_ref)
        return carry

    lax.fori_loop(0, STEPS, body, 0, unroll=UNROLL)


def field_step(block, step, tables_ref, phases_ref, vec_ref, out_ref):
    table = tables_ref[block]
    plus, minus = [], []
    for face in range(4):
        vec = vec_ref[pl.ds(face * FACE, FACE), :]
        both = jnp.dot(table, vec, preferred_element_type=F32)
        cos_real, cos_imag = both[:STEP_ROWS, :PORTS], both[:STEP_ROWS, PORTS:]
        sin_real, sin_imag = both[STEP_ROWS:, :PORTS], both[STEP_ROWS:, PORTS:]
        plus.append((cos_real + sin_imag, cos_imag - sin_real))
        minus.append((cos_real - sin_imag, cos_imag + sin_real))
    phases = phases_ref[block].T
    quarter = HALF_PHIS // 2
    for theta in range(STEP_THETAS):
        low = theta * HALF_PHIS
        high = low + HALF_PHIS

        def along_y(face, part):
            return (plus[face][part][low:high], minus[face][part][low:high])

        def along_x(face, part):
            first, second = plus[face][part][low:high], minus[face][part][low:high]
            return (
                jnp.concatenate([first[quarter:], second[:quarter]], axis=0),
                jnp.concatenate([second[quarter:], first[:quarter]], axis=0),
            )

        kinds = (along_y, along_y, along_x, along_x)
        terms = [[kind(face, part) for part in (0, 1)] for face, kind in enumerate(kinds)]
        for half in range(2):
            start = theta * PHIS + half * HALF_PHIS
            cols = phases[start : start + HALF_PHIS]
            shared = [terms[0][part][half] + terms[2][part][half] for part in (0, 1)]
            real, imag = 0.0, 0.0
            for column, (re, im) in (
                (0, shared),
                (2, (terms[1][0][half], terms[1][1][half])),
                (4, (terms[3][0][half], terms[3][1][half])),
            ):
                cos, sin = cols[:, column : column + 1], cols[:, column + 1 : column + 2]
                real = real + cos * re + sin * im
                imag = imag + cos * im - sin * re
            rows = pl.ds(pl.multiple_of(step * STEP_DIRS + start, HALF_PHIS), HALF_PHIS)
            out_ref[rows, :PORTS] = real.astype(BF16)
            out_ref[rows, PORTS:] = imag.astype(BF16)


def call(kernel, inputs, outputs, scratch, in_space, out_space, flops, moved):
    return pl.pallas_call(
        kernel,
        out_shape=outputs,
        in_specs=[pl.BlockSpec(memory_space=in_space.get(i, VMEM)) for i in range(len(inputs))],
        out_specs=[pl.BlockSpec(memory_space=out_space.get(i, VMEM)) for i in range(len(outputs))],
        scratch_shapes=scratch,
        compiler_params=pltpu.CompilerParams(vmem_limit_bytes=VMEM_LIMIT),
        cost_estimate=pl.CostEstimate(flops=flops, bytes_accessed=moved, transcendentals=0),
    )(*inputs)


def shape(dims, dtype):
    return jax.ShapeDtypeStruct(dims, dtype)


def pairings(count):
    near = [(i, i ^ 1) for i in range(count)]
    far = [(i, (i + 1) % count if i % 2 else (i - 1) % count) for i in range(count)]
    return far, near


def send(kind, axis, value):
    permutation = pairings(lax.axis_size(axis))[kind]
    return lax.ppermute(value, axis, permutation)


def exchange(first_sends, second_call):
    received = [send(kind, "gy", value) for kind, value in enumerate(first_sends)]
    rest = []
    for kind in range(2):
        value, *more = second_call(2 + kind)
        rest += more
        received.append(send(kind, "gx", value))
    return received, rest


def phase_kernel(place_ref, cosines_ref, out_ref):
    factor = 1.0 / math.sqrt(ORDER * lax.axis_size("gx") * lax.axis_size("gy"))
    dir_x, dir_y = cosines_ref[:, 0], cosines_ref[:, 1]
    place_x, place_y = place_ref[0].astype(F32), place_ref[1].astype(F32)
    for index, (extra_x, extra_y) in enumerate(((0.0, 0.0), (SPACING, 0.0), (0.0, SPACING))):
        turns = ((place_x + extra_x) * dir_x + (place_y + extra_y) * dir_y) / WAVE
        angle = (turns - jnp.round(turns)) * (2.0 * math.pi)
        out_ref[:, 2 * index] = jnp.cos(angle) * factor
        out_ref[:, 2 * index + 1] = jnp.sin(angle) * factor
    for index in (6, 7):
        out_ref[:, index] = jnp.zeros((2 * STEPS, STEP_DIRS), F32)


def local(operator, incident, feed, port_element, positions):
    count_x, count_y = lax.axis_size("gx"), lax.axis_size("gy")
    half_flops = 2 * ORDER * ORDER * WIDE
    field_flops = 2 * ANGLES // 2 * FACE * WIDE * 4
    face_pair = [shape((FACE, WIDE), BF16)] * 2
    base_pair = shape((2, FACE, WIDE), F32)
    wide_bf16 = shape((ORDER, WIDE), BF16)
    oper, rhs, base_first, *sends = call(
        base_first_kernel,
        [
            pltpu.with_memory_space_constraint(value, HBM)
            for value in (operator[0, 0], incident[0, 0], feed[0, 0], port_element.reshape(1, PORTS))
        ],
        [shape((4, 2, FACE, ORDER), BF16), wide_bf16, base_pair] + face_pair,
        [
            VMEM((2, ORDER, PORTS), BF16),
            VMEM((2, ORDER), BF16),
            VMEM((1, PORTS), jnp.int32),
            VMEM((ORDER, WIDE), BF16),
            pltpu.SemaphoreType.DMA((4, 4)),
            pltpu.SemaphoreType.DMA((3,)),
        ],
        {0: HBM, 1: HBM, 2: HBM, 3: HBM},
        {},
        half_flops,
        10_000_000,
    )

    def second_base(slot):
        base, out = call(
            functools.partial(base_second_kernel, slot),
            (oper, rhs),
            [shape((1, FACE, WIDE), F32), face_pair[0]],
            [],
            {},
            {},
            half_flops // 2,
            2_500_000,
        )
        return out, base

    received, bases = exchange(sends, second_base)
    far_bf16 = shape((2 * FACE, WIDE), BF16)

    def near_part(received):
        return call(
            near_kernel,
            (oper, base_first, *bases, received[1], received[3]),
            [base_pair] * 2,
            [],
            {},
            {},
            half_flops,
            5_000_000,
        )

    for _ in range(1, ITERS):
        part_first, part_second = near_part(received)
        *sends, trace = call(
            step_first_kernel,
            (oper, part_first, received[0], received[2]),
            face_pair + [far_bf16],
            [],
            {},
            {},
            half_flops // 2,
            2_500_000,
        )
        received, _ = exchange(
            sends,
            lambda slot: call(
                functools.partial(step_second_kernel, slot),
                (oper, part_second, trace),
                face_pair[:1],
                [],
                {},
                {},
                half_flops // 4,
                1_250_000,
            ),
        )
    part_first, part_second = near_part(received)
    (phases,) = call(
        phase_kernel,
        (positions.reshape(2), jnp.asarray(direction_cosines())),
        [shape((2 * STEPS, 8, STEP_DIRS), F32)],
        [],
        {0: pltpu.SMEM},
        {},
        1_000_000,
        100_000,
    )
    tables = jnp.asarray(face_tables())
    half_field = shape((ANGLES // 2, WIDE), BF16)
    currents, vec, theirs = call(
        last_kernel,
        (oper, part_first, part_second, *received, tables, phases),
        [shape((2, ORDER, PORTS), BF16), wide_bf16, half_field],
        [VMEM((2, ORDER, PORTS), BF16), pltpu.SemaphoreType.DMA],
        {},
        {0: HBM},
        half_flops + field_flops,
        2_000_000,
    )
    theirs = lax.ppermute(theirs, "gx", [(i, i ^ 1) for i in range(count_x)])
    (mine,) = call(own_field_kernel, (tables, phases, vec), [half_field], [], {}, {}, field_flops, 1_000_000)
    pair = (mine.astype(F32) + theirs.astype(F32)).astype(BF16)
    runs = 2
    length = count_y // runs
    across = [
        [i * count_y + run * length + at for i in range(parity, count_x, 2) for run in range(runs)]
        for parity in (0, 1)
        for at in range(length)
    ]
    along = [[run * length + at for at in range(length)] for run in range(runs)]
    members = len(across[0])
    pieces = lax.all_to_all(pair, ("gx", "gy"), 0, 0, tiled=True, axis_index_groups=across)
    column = jnp.sum(pieces.reshape(members, -1, WIDE).astype(F32), axis=0).astype(BF16)
    pieces = lax.all_to_all(column, "gy", 0, 0, tiled=True, axis_index_groups=along)
    pieces = pieces.reshape(length, -1, WIDE).astype(F32)
    fields = jnp.stack([jnp.sum(pieces[..., :PORTS], axis=0), jnp.sum(pieces[..., PORTS:], axis=0)], axis=1)
    return (currents[None, None], fields)


def solution(mesh):
    return jax.shard_map(
        local,
        mesh=mesh,
        in_specs=(
            P("gx", "gy", None, None, None),
            P("gx", "gy", None, None, None),
            P("gx", "gy", None, None),
            P(),
            P("gx", "gy", None),
        ),
        out_specs=(P("gx", "gy", None, None, None), P(("gx", "gy"), None, None)),
        check_vma=False,
    )
```

profile of v0, /device:TPU:2, one launch (start us, length us, event | category | flops | bytes accessed | tf_op | source)
XLA Modules:
  0.0 87.5 jit_solution(17859798937050539703)
XLA Ops:
  0.6 5.2 %shard_map.86 = (bf16[4,2,384,1536]{3,2,1,0:T(8,128)(2,1)S(1)}, bf16[1536,256]{1,0:T(8,128)(2,1)S(1)}, f32[2,384,256]{2,1,0:T(8,128)S(1)}, bf16[384,256]{1,0:T(8,128)(2,1)S(1)}, bf16[384,256]{1,0:T(8,128)(2,1)S(1)}) custom-call(bf16[2,1536,1536]{2,1,0:T(8,128)(2,1)} %bitcast.11, bf16[2,1536,128]{2,1,0:T(8,128)(2,1)} %bitcast.13, bf16[2,1536]{1,0:T(2,128)(2,1)} %bitcast.17, ...), custom_call_target="tpu_custom_call" | custom-call | flops 1207959552 | bytes 10000000 | tf_op jit(solution)/shard_map/pallas_call | solution.py:268
  5.8 2.0 %collective-permute-start = (bf16[384,256]{1,0:T(8,128)(2,1)S(1)}, bf16[384,256]{1,0:T(8,128)(2,1)S(1)}, u32[]{:S(2)}, u32[]{:S(2)}) collective-permute-start(bf16[384,256]{1,0:T(8,128)(2,1)S(1)} %get-tuple-element.31), channel_id=1, source_target_pairs={{0,1},{1,0},{2,3},{3,2},{4,5},{5,4},{6,7},{7,6},{8,9},{9,8},{10,11... | collective-permute-start | bytes 589832 | tf_op jit(solution)/shard_map/ppermute | solution.py:291
  7.8 0.8 shard_map.88
  8.7 7.7 %collective-permute-start.2 = (bf16[384,256]{1,0:T(8,128)(2,1)S(1)}, bf16[384,256]{1,0:T(8,128)(2,1)S(1)}, u32[]{:S(2)}, u32[]{:S(2)}) collective-permute-start(bf16[384,256]{1,0:T(8,128)(2,1)S(1)} %get-tuple-element.34), channel_id=1, source_target_pairs={{0,15},{1,2},{2,1},{3,4},{4,3},{5,6},{6,5},{7,8},{8,7},{9,10},{10,... | collective-permute-start | bytes 589832 | tf_op jit(solution)/shard_map/ppermute | solution.py:291
  16.4 0.8 shard_map.87
  17.1 0.4 collective-permute-start.3
  17.5 1.4 %shard_map.89 = (f32[2,384,256]{2,1,0:T(8,128)S(1)}, f32[2,384,256]{2,1,0:T(8,128)S(1)}) custom-call(bf16[4,2,384,1536]{3,2,1,0:T(8,128)(2,1)S(1)} %get-tuple-element.26.oper_ref, f32[2,384,256]{2,1,0:T(8,128)S(1)} %get-tuple-element.27.base_first_ref, f32[1,384,256]{2,1,0:T(8,128)S(1)} %get-tuple-element.29.base_second_ref, ...), custom_call_target="tpu_custom_call" | custom-call | flops 1207959552 | bytes 5000000 | tf_op jit(solution)/shard_map/pallas_call | solution.py:268
  18.9 2.9 %collective-permute-done.2.far_y_ref = bf16[384,256]{1,0:T(8,128)(2,1)S(1)} collective-permute-done((bf16[384,256]{1,0:T(8,128)(2,1)S(1)}, bf16[384,256]{1,0:T(8,128)(2,1)S(1)}, u32[]{:S(2)}, u32[]{:S(2)}) %collective-permute-start.2) | collective-permute-done | bytes 196640 | tf_op jit(solution)/shard_map/ppermute | solution.py:291
  21.8 0.5 collective-permute-done.3.far_x_ref
  22.3 0.8 shard_map.90
  23.1 0.5 shard_map.91
  23.6 0.2 collective-permute-start.5
  23.8 0.5 shard_map.93
  24.3 2.7 %collective-permute-start.7 = (bf16[384,256]{1,0:T(8,128)(2,1)S(1)}, bf16[384,256]{1,0:T(8,128)(2,1)S(1)}, u32[]{:S(2)}, u32[]{:S(2)}) collective-permute-start(bf16[384,256]{1,0:T(8,128)(2,1)S(1)} %shard_map.93), channel_id=1, source_target_pairs={{0,240},{16,32},{32,16},{48,64},{64,48},{80,96},{96,80},{112,128},... | collective-permute-start | bytes 589832 | tf_op jit(solution)/shard_map/ppermute | solution.py:291
  27.0 4.1 %collective-permute-start.6 = (bf16[384,256]{1,0:T(8,128)(2,1)S(1)}, bf16[384,256]{1,0:T(8,128)(2,1)S(1)}, u32[]{:S(2)}, u32[]{:S(2)}) collective-permute-start(bf16[384,256]{1,0:T(8,128)(2,1)S(1)} %get-tuple-element.40), channel_id=1, source_target_pairs={{0,15},{1,2},{2,1},{3,4},{4,3},{5,6},{6,5},{7,8},{8,7},{9,10},{10,... | collective-permute-start | bytes 589832 | tf_op jit(solution)/shard_map/ppermute | solution.py:291
  31.1 1.4 %shard_map.92 = (f32[2,384,256]{2,1,0:T(8,128)S(1)}, f32[2,384,256]{2,1,0:T(8,128)S(1)}) custom-call(bf16[4,2,384,1536]{3,2,1,0:T(8,128)(2,1)S(1)} %get-tuple-element.26.oper_ref, f32[2,384,256]{2,1,0:T(8,128)S(1)} %get-tuple-element.27.base_first_ref, f32[1,384,256]{2,1,0:T(8,128)S(1)} %get-tuple-element.29.base_second_ref, ...), custom_call_target="tpu_custom_call" | custom-call | flops 1207959552 | bytes 5000000 | tf_op jit(solution)/shard_map/pallas_call | solution.py:268
  32.5 3.9 %collective-permute-done.6.far_y_ref = bf16[384,256]{1,0:T(8,128)(2,1)S(1)} collective-permute-done((bf16[384,256]{1,0:T(8,128)(2,1)S(1)}, bf16[384,256]{1,0:T(8,128)(2,1)S(1)}, u32[]{:S(2)}, u32[]{:S(2)}) %collective-permute-start.6) | collective-permute-done | bytes 196640 | tf_op jit(solution)/shard_map/ppermute | solution.py:291
  36.4 0.8 shard_map.94
  37.2 0.5 shard_map.95
  37.8 0.3 collective-permute-start.8
  38.1 0.5 shard_map.97
  38.6 2.5 %collective-permute-start.11 = (bf16[384,256]{1,0:T(8,128)(2,1)S(1)}, bf16[384,256]{1,0:T(8,128)(2,1)S(1)}, u32[]{:S(2)}, u32[]{:S(2)}) collective-permute-start(bf16[384,256]{1,0:T(8,128)(2,1)S(1)} %shard_map.97), channel_id=1, source_target_pairs={{0,240},{16,32},{32,16},{48,64},{64,48},{80,96},{96,80},{112,128},... | collective-permute-start | bytes 589832 | tf_op jit(solution)/shard_map/ppermute | solution.py:291
  41.1 5.6 %collective-permute-start.10 = (bf16[384,256]{1,0:T(8,128)(2,1)S(1)}, bf16[384,256]{1,0:T(8,128)(2,1)S(1)}, u32[]{:S(2)}, u32[]{:S(2)}) collective-permute-start(bf16[384,256]{1,0:T(8,128)(2,1)S(1)} %get-tuple-element.46), channel_id=1, source_target_pairs={{0,15},{1,2},{2,1},{3,4},{4,3},{5,6},{6,5},{7,8},{8,7},{9,10},{10,... | collective-permute-start | bytes 589832 | tf_op jit(solution)/shard_map/ppermute | solution.py:291
  46.7 0.9 %shard_map.98.rest_5_.phases_ref = f32[8,8,256]{2,1,0:T(8,128)S(1)} custom-call(s32[2]{0:T(128)S(1)} %bitcast.10, f32[8,2,256]{2,1,0:T(2,128)S(1)} %copy-done.1), custom_call_target="tpu_custom_call" | custom-call | flops 1000000 | bytes 100000 | tf_op jit(solution)/shard_map/pallas_call | solution.py:268
  47.7 1.4 %shard_map.96 = (f32[2,384,256]{2,1,0:T(8,128)S(1)}, f32[2,384,256]{2,1,0:T(8,128)S(1)}) custom-call(bf16[4,2,384,1536]{3,2,1,0:T(8,128)(2,1)S(1)} %get-tuple-element.26.oper_ref, f32[2,384,256]{2,1,0:T(8,128)S(1)} %get-tuple-element.27.base_first_ref, f32[1,384,256]{2,1,0:T(8,128)S(1)} %get-tuple-element.29.base_second_ref, ...), custom_call_target="tpu_custom_call" | custom-call | flops 1207959552 | bytes 5000000 | tf_op jit(solution)/shard_map/pallas_call | solution.py:268
  49.1 1.3 %collective-permute-done.10.rest_0_ = bf16[384,256]{1,0:T(8,128)(2,1)S(1)} collective-permute-done((bf16[384,256]{1,0:T(8,128)(2,1)S(1)}, bf16[384,256]{1,0:T(8,128)(2,1)S(1)}, u32[]{:S(2)}, u32[]{:S(2)}) %collective-permute-start.10) | collective-permute-done | bytes 196640 | tf_op jit(solution)/shard_map/ppermute | solution.py:291
  50.3 3.0 %shard_map.99 = (bf16[2,1536,128]{2,1,0:T(8,128)(2,1)}, bf16[1536,256]{1,0:T(8,128)(2,1)S(1)}, bf16[1024,256]{1,0:T(8,128)(2,1)S(1)}) custom-call(bf16[4,2,384,1536]{3,2,1,0:T(8,128)(2,1)S(1)} %get-tuple-element.26.oper_ref, f32[2,384,256]{2,1,0:T(8,128)S(1)} %get-tuple-element.44.part_first_ref, f32[2,384,256]{2,1,0:T(8,128)S(1)} %get-tuple-element.45.part_second_ref, ...), custom_call_target="tpu_custom_call" | custom-call | flops 2013265920 | bytes 2000000 | tf_op jit(solution)/shard_map/pallas_call | solution.py:268
  53.5 1.7 %shard_map.100 = bf16[1024,256]{1,0:T(8,128)(2,1)S(1)} custom-call(bf16[8,256,384]{2,1,0:T(8,128)(2,1)S(1)} %copy-done, f32[8,8,256]{2,1,0:T(8,128)S(1)} %shard_map.98.rest_5_.phases_ref, bf16[1536,256]{1,0:T(8,128)(2,1)S(1)} %get-tuple-element.48.vec_ref), custom_call_target="tpu_custom_call" | custom-call | flops 805306368 | bytes 1000000 | tf_op jit(solution)/shard_map/pallas_call | solution.py:268
  55.2 0.2 collective-permute-done.12
  55.5 19.4 %all_to_all.18 = bf16[16,64,256]{2,1,0:T(8,128)(2,1)S(1)} all-to-all(bf16[16,64,256]{2,1,0:T(8,128)(2,1)S(1)} %bitcast.12), channel_id=1, replica_groups={{0,8,32,40,64,72,96,104,128,136,160,168,192,200,224,232},{1,9,33,41,65,..., dimensions={0} | all-to-all | bytes 1048576 | tf_op jit(solution)/shard_map/all_to_all | solution.py:433
  75.0 11.9 %all_to_all.19 = bf16[8,8,256]{2,1,0:T(8,128)(2,1)S(1)} all-to-all(bf16[8,8,256]{2,1,0:T(8,128)(2,1)S(1)} %bitcast.14), channel_id=1, replica_groups={{0,1,2,3,4,5,6,7},{8,9,10,11,12,13,14,15},{16,17,18,19,20,21,22,23},{24..., dimensions={0} | all-to-all | bytes 65536 | tf_op jit(solution)/shard_map/all_to_all | solution.py:435
  86.9 0.6 copy.9
  (23 shorter events, 0.6 us)
Async XLA Ops:
  5.8 11.7 %collective-permute-start = (bf16[384,256]{1,0:T(8,128)(2,1)S(1)}, bf16[384,256]{1,0:T(8,128)(2,1)S(1)}, u32[]{:S(2)}, u32[]{:S(2)}) collective-permute-start(bf16[384,256]{1,0:T(8,128)(2,1)S(1)} %get-tuple-element.31), channel_id=1, source_target_pairs={{0,1},{1,0},{2,3},{3,2},{4,5},{5,4},{6,7},{7,6},{8,9},{9,8},{10,11... | collective-permute-start | bytes 589832 | tf_op jit(solution)/shard_map/ppermute | solution.py:291
  8.6 8.9 %collective-permute-start.1 = (bf16[384,256]{1,0:T(8,128)(2,1)S(1)}, bf16[384,256]{1,0:T(8,128)(2,1)S(1)}, u32[]{:S(2)}, u32[]{:S(2)}) collective-permute-start(bf16[384,256]{1,0:T(8,128)(2,1)S(1)} %get-tuple-element.32), channel_id=1, source_target_pairs={{0,16},{16,0},{32,48},{48,32},{64,80},{80,64},{96,112},{112,96},{1... | collective-permute-start | bytes 589832 | tf_op jit(solution)/shard_map/ppermute | solution.py:291
  8.7 13.1 %collective-permute-start.2 = (bf16[384,256]{1,0:T(8,128)(2,1)S(1)}, bf16[384,256]{1,0:T(8,128)(2,1)S(1)}, u32[]{:S(2)}, u32[]{:S(2)}) collective-permute-start(bf16[384,256]{1,0:T(8,128)(2,1)S(1)} %get-tuple-element.34), channel_id=1, source_target_pairs={{0,15},{1,2},{2,1},{3,4},{4,3},{5,6},{6,5},{7,8},{8,7},{9,10},{10,... | collective-permute-start | bytes 589832 | tf_op jit(solution)/shard_map/ppermute | solution.py:291
  17.1 5.2 %collective-permute-start.3 = (bf16[384,256]{1,0:T(8,128)(2,1)S(1)}, bf16[384,256]{1,0:T(8,128)(2,1)S(1)}, u32[]{:S(2)}, u32[]{:S(2)}) collective-permute-start(bf16[384,256]{1,0:T(8,128)(2,1)S(1)} %get-tuple-element.35), channel_id=1, source_target_pairs={{0,240},{16,32},{32,16},{48,64},{64,48},{80,96},{96,80},{112,128},... | collective-permute-start | bytes 589832 | tf_op jit(solution)/shard_map/ppermute | solution.py:291
  23.6 7.5 %collective-permute-start.5 = (bf16[384,256]{1,0:T(8,128)(2,1)S(1)}, bf16[384,256]{1,0:T(8,128)(2,1)S(1)}, u32[]{:S(2)}, u32[]{:S(2)}) collective-permute-start(bf16[384,256]{1,0:T(8,128)(2,1)S(1)} %shard_map.91), channel_id=1, source_target_pairs={{0,16},{16,0},{32,48},{48,32},{64,80},{80,64},{96,112},{112,96},{1... | collective-permute-start | bytes 589832 | tf_op jit(solution)/shard_map/ppermute | solution.py:291
  23.8 7.3 %collective-permute-start.4 = (bf16[384,256]{1,0:T(8,128)(2,1)S(1)}, bf16[384,256]{1,0:T(8,128)(2,1)S(1)}, u32[]{:S(2)}, u32[]{:S(2)}) collective-permute-start(bf16[384,256]{1,0:T(8,128)(2,1)S(1)} %get-tuple-element.36), channel_id=1, source_target_pairs={{0,1},{1,0},{2,3},{3,2},{4,5},{5,4},{6,7},{7,6},{8,9},{9,8},{10,11... | collective-permute-start | bytes 589832 | tf_op jit(solution)/shard_map/ppermute | solution.py:291
  24.3 8.2 %collective-permute-start.7 = (bf16[384,256]{1,0:T(8,128)(2,1)S(1)}, bf16[384,256]{1,0:T(8,128)(2,1)S(1)}, u32[]{:S(2)}, u32[]{:S(2)}) collective-permute-start(bf16[384,256]{1,0:T(8,128)(2,1)S(1)} %shard_map.93), channel_id=1, source_target_pairs={{0,240},{16,32},{32,16},{48,64},{64,48},{80,96},{96,80},{112,128},... | collective-permute-start | bytes 589832 | tf_op jit(solution)/shard_map/ppermute | solution.py:291
  27.0 9.4 %collective-permute-start.6 = (bf16[384,256]{1,0:T(8,128)(2,1)S(1)}, bf16[384,256]{1,0:T(8,128)(2,1)S(1)}, u32[]{:S(2)}, u32[]{:S(2)}) collective-permute-start(bf16[384,256]{1,0:T(8,128)(2,1)S(1)} %get-tuple-element.40), channel_id=1, source_target_pairs={{0,15},{1,2},{2,1},{3,4},{4,3},{5,6},{6,5},{7,8},{8,7},{9,10},{10,... | collective-permute-start | bytes 589832 | tf_op jit(solution)/shard_map/ppermute | solution.py:291
  37.2 9.5 %copy-start.1 = (f32[8,2,256]{2,1,0:T(2,128)S(1)}, f32[8,2,256]{2,1,0:T(2,128)}, u32[]{:S(2)}) copy-start(f32[8,2,256]{2,1,0:T(2,128)} %constant.8.clone.cosines_ref) | copy-start | bytes 49156
  37.2 9.5 %copy-start.2 = (s32[1,1,2]{2,1,0:T(1,128)S(1)}, s32[1,1,2]{2,1,0:T(1,128)}, u32[]{:S(2)}) copy-start(s32[1,1,2]{2,1,0:T(1,128)} %param.11) | copy-start | bytes 28
  37.7 9.9 %collective-permute-start.9 = (bf16[384,256]{1,0:T(8,128)(2,1)S(1)}, bf16[384,256]{1,0:T(8,128)(2,1)S(1)}, u32[]{:S(2)}, u32[]{:S(2)}) collective-permute-start(bf16[384,256]{1,0:T(8,128)(2,1)S(1)} %shard_map.95), channel_id=1, source_target_pairs={{0,16},{16,0},{32,48},{48,32},{64,80},{80,64},{96,112},{112,96},{1... | collective-permute-start | bytes 589832 | tf_op jit(solution)/shard_map/ppermute | solution.py:291
  37.8 12.6 %copy-start = (bf16[8,256,384]{2,1,0:T(8,128)(2,1)S(1)}, bf16[8,256,384]{2,1,0:T(8,128)(2,1)}, u32[]{:S(2)}) copy-start(bf16[8,256,384]{2,1,0:T(8,128)(2,1)} %constant.9.clone.rest_4_.tables_ref) | copy-start | bytes 4718596
  37.8 9.8 %collective-permute-start.8 = (bf16[384,256]{1,0:T(8,128)(2,1)S(1)}, bf16[384,256]{1,0:T(8,128)(2,1)S(1)}, u32[]{:S(2)}, u32[]{:S(2)}) collective-permute-start(bf16[384,256]{1,0:T(8,128)(2,1)S(1)} %get-tuple-element.41), channel_id=1, source_target_pairs={{0,1},{1,0},{2,3},{3,2},{4,5},{5,4},{6,7},{7,6},{8,9},{9,8},{10,11... | collective-permute-start | bytes 589832 | tf_op jit(solution)/shard_map/ppermute | solution.py:291
  38.6 10.5 %collective-permute-start.11 = (bf16[384,256]{1,0:T(8,128)(2,1)S(1)}, bf16[384,256]{1,0:T(8,128)(2,1)S(1)}, u32[]{:S(2)}, u32[]{:S(2)}) collective-permute-start(bf16[384,256]{1,0:T(8,128)(2,1)S(1)} %shard_map.97), channel_id=1, source_target_pairs={{0,240},{16,32},{32,16},{48,64},{64,48},{80,96},{96,80},{112,128},... | collective-permute-start | bytes 589832 | tf_op jit(solution)/shard_map/ppermute | solution.py:291
  41.1 9.3 %collective-permute-start.10 = (bf16[384,256]{1,0:T(8,128)(2,1)S(1)}, bf16[384,256]{1,0:T(8,128)(2,1)S(1)}, u32[]{:S(2)}, u32[]{:S(2)}) collective-permute-start(bf16[384,256]{1,0:T(8,128)(2,1)S(1)} %get-tuple-element.46), channel_id=1, source_target_pairs={{0,15},{1,2},{2,1},{3,4},{4,3},{5,6},{6,5},{7,8},{8,7},{9,10},{10,... | collective-permute-start | bytes 589832 | tf_op jit(solution)/shard_map/ppermute | solution.py:291
  53.4 2.0 %collective-permute-start.12 = (bf16[1024,256]{1,0:T(8,128)(2,1)S(1)}, bf16[1024,256]{1,0:T(8,128)(2,1)S(1)}, u32[]{:S(2)}, u32[]{:S(2)}) collective-permute-start(bf16[1024,256]{1,0:T(8,128)(2,1)S(1)} %get-tuple-element.49), channel_id=1, source_target_pairs={{0,16},{16,0},{32,48},{48,32},{64,80},{80,64},{96,112},{112,96},{1... | collective-permute-start | bytes 1572872 | tf_op jit(solution)/shard_map/ppermute | solution.py:421
where the time goes:
time: 87.7 us; the launch traced here: 87.5 us
  blocking collectives  31.3 us (36%)
  starting transfers between devices  25.8 us (29%)
  Pallas kernels  20 us (23%)
  waiting for transfers between devices  8.8 us (10%)
    ppermute x12, starting transfers between devices, send(): return lax.ppermute(value, axis, permutation)  25.7 us
    pallas_call x15, Pallas kernels, call(): pl.pallas_call(kernel, out_shape=outputs, in_specs=[pl.BlockSpec(memory_s...  20 us
    all_to_all x1, blocking collectives, local(): lax.all_to_all(pair, ('gx', 'gy'), 0, 0, tiled=True, axis_index_groups=ac...  19.4 us
    all_to_all x1, blocking collectives, local(): lax.all_to_all(column, 'gy', 0, 0, tiled=True, axis_index_groups=along)  11.9 us
    ppermute x12, waiting for transfers between devices, send(): return lax.ppermute(value, axis, permutation)  8.6 us
  transfers between devices with their start and end apart: 13, of which 5 were waited for; matrix products, arithmetic and copies ran while one was open for 0% of the time, Pallas kernels for 11%

commit v1 on v0

--- a/solution.py
+++ b/solution.py
@@ -87,6 +87,8 @@
 ALL_COLS = slice(0, ORDER)
 NEAR_COLS = slice(0, 2 * FACE)
 FAR_COLS = slice(2 * FACE, ORDER)
+FAR_Y_COLS = slice(2 * FACE, 3 * FACE)
+FAR_X_COLS = slice(3 * FACE, ORDER)
 
 
 def base_first_kernel(oper_hbm, incident_hbm, feed_hbm, ports_hbm, oper_ref, rhs_ref, base_ref, *rest):
@@ -188,14 +190,23 @@
     out_ref[...] = (2.0 * (part_ref[slot - 2] + coupled)).astype(BF16)
 
 
+def far_y_kernel(oper_ref, part_first_ref, part_second_ref, far_y_ref, *outs):
+    trace = far_y_ref[...]
+    trace_swapped = swapped(trace)
+    for slot in range(4):
+        part = (part_first_ref if slot < 2 else part_second_ref)[slot % 2]
+        outs[slot // 2][slot % 2] = part + slot_product(oper_ref, slot, FAR_Y_COLS, trace, trace_swapped)
+
+
 def last_kernel(oper_ref, part_first_ref, part_second_ref, *rest):
     traces, tables_ref, phases_ref = rest[:4], rest[4], rest[5]
     currents_hbm, vec_ref, out_ref, split_ref, sem = rest[6:]
-    trace, trace_swapped = joined(traces[0], traces[2])
+    trace = traces[2][...]
+    trace_swapped = swapped(trace)
     for slot, face in enumerate(faces_in_order()):
         rows = face_rows(face)
         part = (part_first_ref if slot < 2 else part_second_ref)[slot % 2]
-        coupled = slot_product(oper_ref, slot, FAR_COLS, trace, trace_swapped)
+        coupled = slot_product(oper_ref, slot, FAR_X_COLS, trace, trace_swapped)
         currents = (part + 0.5 * traces[slot][...].astype(F32) + coupled).astype(BF16)
         vec_ref[rows, :] = currents
         split_ref[0, rows, :] = currents[:, :PORTS]
@@ -396,6 +407,16 @@
             ),
         )
     part_first, part_second = near_part(received)
+    part_first, part_second = call(
+        far_y_kernel,
+        (oper, part_first, part_second, received[0]),
+        [base_pair] * 2,
+        [],
+        {},
+        {},
+        half_flops // 2,
+        2_500_000,
+    )
     (phases,) = call(
         phase_kernel,
         (positions.reshape(2), jnp.asarray(direction_cosines())),

time: 87.7 us -> 88.1 us (level)
  waiting for transfers between devices: 8.8 us -> 7.51 us
  blocking collectives: 31.3 us -> 32.5 us
    all_to_all x1, blocking collectives: 11.9 us -> 13.7 us  [local(): lax.all_to_all(column, 'gy', 0, 0, tiled=True, axis_index_groups=along)]
    ppermute x12, waiting for transfers between devices: 8.6 us -> 7.32 us  [send(): return lax.ppermute(value, axis, permutation)]
    pallas_call x15 -> x16, Pallas kernels: 20 us -> 20.6 us  [call(): pl.pallas_call(kernel, out_shape=outputs, in_specs=[pl.BlockSpec(memory_s...]
  transfers between devices with their start and end apart: 13 -> 13, of which waited for: 5 -> 4; matrix products, arithmetic and copies ran while one was open for 0% -> 0% of each run, Pallas kernels for 11% -> 12%
where the time goes in v1:
time: 88.1 us; the launch traced here: 87.9 us
  blocking collectives  32.5 us (37%)
  starting transfers between devices  25.5 us (29%)
  Pallas kernels  20.6 us (23%)
  waiting for transfers between devices  7.51 us (9%)
    ppermute x12, starting transfers between devices, send(): return lax.ppermute(value, axis, permutation)  25.4 us
    pallas_call x16, Pallas kernels, call(): pl.pallas_call(kernel, out_shape=outputs, in_specs=[pl.BlockSpec(memory_s...  20.6 us
    all_to_all x1, blocking collectives, local(): lax.all_to_all(pair, ('gx', 'gy'), 0, 0, tiled=True, axis_index_groups=ac...  18.9 us
    all_to_all x1, blocking collectives, local(): lax.all_to_all(column, 'gy', 0, 0, tiled=True, axis_index_groups=along)  13.7 us
    ppermute x12, waiting for transfers between devices, send(): return lax.ppermute(value, axis, permutation)  7.32 us
  transfers between devices with their start and end apart: 13, of which 4 were waited for; matrix products, arithmetic and copies ran while one was open for 0% of the time, Pallas kernels for 12%

profile of v1, /device:TPU:2, one launch (start us, length us, event | category | flops | bytes accessed | tf_op | source)
XLA Modules:
  0.0 87.9 jit_solution(17276193814046704329)
XLA Ops:
  0.6 5.2 %shard_map.86 = (bf16[4,2,384,1536]{3,2,1,0:T(8,128)(2,1)S(1)}, bf16[1536,256]{1,0:T(8,128)(2,1)S(1)}, f32[2,384,256]{2,1,0:T(8,128)S(1)}, bf16[384,256]{1,0:T(8,128)(2,1)S(1)}, bf16[384,256]{1,0:T(8,128)(2,1)S(1)}) custom-call(bf16[2,1536,1536]{2,1,0:T(8,128)(2,1)} %bitcast.11, bf16[2,1536,128]{2,1,0:T(8,128)(2,1)} %bitcast.13, bf16[2,1536]{1,0:T(2,128)(2,1)} %bitcast.17, ...), custom_call_target="tpu_custom_call" | custom-call | flops 1207959552 | bytes 10000000 | tf_op jit(solution)/shard_map/pallas_call | solution.py:279
  5.8 2.0 %collective-permute-start = (bf16[384,256]{1,0:T(8,128)(2,1)S(1)}, bf16[384,256]{1,0:T(8,128)(2,1)S(1)}, u32[]{:S(2)}, u32[]{:S(2)}) collective-permute-start(bf16[384,256]{1,0:T(8,128)(2,1)S(1)} %get-tuple-element.33), channel_id=1, source_target_pairs={{0,1},{1,0},{2,3},{3,2},{4,5},{5,4},{6,7},{7,6},{8,9},{9,8},{10,11... | collective-permute-start | bytes 589832 | tf_op jit(solution)/shard_map/ppermute | solution.py:302
  7.8 0.8 shard_map.88
  8.7 7.7 %collective-permute-start.2 = (bf16[384,256]{1,0:T(8,128)(2,1)S(1)}, bf16[384,256]{1,0:T(8,128)(2,1)S(1)}, u32[]{:S(2)}, u32[]{:S(2)}) collective-permute-start(bf16[384,256]{1,0:T(8,128)(2,1)S(1)} %get-tuple-element.36), channel_id=1, source_target_pairs={{0,15},{1,2},{2,1},{3,4},{4,3},{5,6},{6,5},{7,8},{8,7},{9,10},{10,... | collective-permute-start | bytes 589832 | tf_op jit(solution)/shard_map/ppermute | solution.py:302
  16.4 0.8 shard_map.87
  17.1 0.4 collective-permute-start.3
  17.5 1.4 %shard_map.89 = (f32[2,384,256]{2,1,0:T(8,128)S(1)}, f32[2,384,256]{2,1,0:T(8,128)S(1)}) custom-call(bf16[4,2,384,1536]{3,2,1,0:T(8,128)(2,1)S(1)} %get-tuple-element.28.oper_ref, f32[2,384,256]{2,1,0:T(8,128)S(1)} %get-tuple-element.29.base_first_ref, f32[1,384,256]{2,1,0:T(8,128)S(1)} %get-tuple-element.31.base_second_ref, ...), custom_call_target="tpu_custom_call" | custom-call | flops 1207959552 | bytes 5000000 | tf_op jit(solution)/shard_map/pallas_call | solution.py:279
  18.9 2.9 %collective-permute-done.2.far_y_ref = bf16[384,256]{1,0:T(8,128)(2,1)S(1)} collective-permute-done((bf16[384,256]{1,0:T(8,128)(2,1)S(1)}, bf16[384,256]{1,0:T(8,128)(2,1)S(1)}, u32[]{:S(2)}, u32[]{:S(2)}) %collective-permute-start.2) | collective-permute-done | bytes 196640 | tf_op jit(solution)/shard_map/ppermute | solution.py:302
  21.8 0.5 collective-permute-done.3.far_x_ref
  22.3 0.8 shard_map.90
  23.1 0.5 shard_map.91
  23.6 0.2 collective-permute-start.5
  23.8 0.5 shard_map.93
  24.3 2.7 %collective-permute-start.7 = (bf16[384,256]{1,0:T(8,128)(2,1)S(1)}, bf16[384,256]{1,0:T(8,128)(2,1)S(1)}, u32[]{:S(2)}, u32[]{:S(2)}) collective-permute-start(bf16[384,256]{1,0:T(8,128)(2,1)S(1)} %shard_map.93), channel_id=1, source_target_pairs={{0,240},{16,32},{32,16},{48,64},{64,48},{80,96},{96,80},{112,128},... | collective-permute-start | bytes 589832 | tf_op jit(solution)/shard_map/ppermute | solution.py:302
  27.0 4.1 %collective-permute-start.6 = (bf16[384,256]{1,0:T(8,128)(2,1)S(1)}, bf16[384,256]{1,0:T(8,128)(2,1)S(1)}, u32[]{:S(2)}, u32[]{:S(2)}) collective-permute-start(bf16[384,256]{1,0:T(8,128)(2,1)S(1)} %get-tuple-element.42), channel_id=1, source_target_pairs={{0,15},{1,2},{2,1},{3,4},{4,3},{5,6},{6,5},{7,8},{8,7},{9,10},{10,... | collective-permute-start | bytes 589832 | tf_op jit(solution)/shard_map/ppermute | solution.py:302
  31.1 1.4 %shard_map.92 = (f32[2,384,256]{2,1,0:T(8,128)S(1)}, f32[2,384,256]{2,1,0:T(8,128)S(1)}) custom-call(bf16[4,2,384,1536]{3,2,1,0:T(8,128)(2,1)S(1)} %get-tuple-element.28.oper_ref, f32[2,384,256]{2,1,0:T(8,128)S(1)} %get-tuple-element.29.base_first_ref, f32[1,384,256]{2,1,0:T(8,128)S(1)} %get-tuple-element.31.base_second_ref, ...), custom_call_target="tpu_custom_call" | custom-call | flops 1207959552 | bytes 5000000 | tf_op jit(solution)/shard_map/pallas_call | solution.py:279
  32.5 3.9 %collective-permute-done.6.far_y_ref = bf16[384,256]{1,0:T(8,128)(2,1)S(1)} collective-permute-done((bf16[384,256]{1,0:T(8,128)(2,1)S(1)}, bf16[384,256]{1,0:T(8,128)(2,1)S(1)}, u32[]{:S(2)}, u32[]{:S(2)}) %collective-permute-start.6) | collective-permute-done | bytes 196640 | tf_op jit(solution)/shard_map/ppermute | solution.py:302
  36.4 0.8 shard_map.94
  37.2 0.5 shard_map.95
  37.8 0.3 collective-permute-start.8
  38.1 4.9 %collective-permute-start.10 = (bf16[384,256]{1,0:T(8,128)(2,1)S(1)}, bf16[384,256]{1,0:T(8,128)(2,1)S(1)}, u32[]{:S(2)}, u32[]{:S(2)}) collective-permute-start(bf16[384,256]{1,0:T(8,128)(2,1)S(1)} %get-tuple-element.48), channel_id=1, source_target_pairs={{0,15},{1,2},{2,1},{3,4},{4,3},{5,6},{6,5},{7,8},{8,7},{9,10},{10,... | collective-permute-start | bytes 589832 | tf_op jit(solution)/shard_map/ppermute | solution.py:302
  43.0 0.5 shard_map.98
  43.5 2.9 %collective-permute-start.11 = (bf16[384,256]{1,0:T(8,128)(2,1)S(1)}, bf16[384,256]{1,0:T(8,128)(2,1)S(1)}, u32[]{:S(2)}, u32[]{:S(2)}) collective-permute-start(bf16[384,256]{1,0:T(8,128)(2,1)S(1)} %shard_map.98), channel_id=1, source_target_pairs={{0,240},{16,32},{32,16},{48,64},{64,48},{80,96},{96,80},{112,128},... | collective-permute-start | bytes 589832 | tf_op jit(solution)/shard_map/ppermute | solution.py:302
  46.4 0.9 %shard_map.99.rest_5_.phases_ref = f32[8,8,256]{2,1,0:T(8,128)S(1)} custom-call(s32[2]{0:T(128)S(1)} %bitcast.10, f32[8,2,256]{2,1,0:T(2,128)S(1)} %copy-done.1), custom_call_target="tpu_custom_call" | custom-call | flops 1000000 | bytes 100000 | tf_op jit(solution)/shard_map/pallas_call | solution.py:279
  47.4 1.4 %shard_map.96 = (f32[2,384,256]{2,1,0:T(8,128)S(1)}, f32[2,384,256]{2,1,0:T(8,128)S(1)}) custom-call(bf16[4,2,384,1536]{3,2,1,0:T(8,128)(2,1)S(1)} %get-tuple-element.28.oper_ref, f32[2,384,256]{2,1,0:T(8,128)S(1)} %get-tuple-element.29.base_first_ref, f32[1,384,256]{2,1,0:T(8,128)S(1)} %get-tuple-element.31.base_second_ref, ...), custom_call_target="tpu_custom_call" | custom-call | flops 1207959552 | bytes 5000000 | tf_op jit(solution)/shard_map/pallas_call | solution.py:279
  48.8 1.0 %shard_map.97 = (f32[2,384,256]{2,1,0:T(8,128)S(1)}, f32[2,384,256]{2,1,0:T(8,128)S(1)}) custom-call(bf16[4,2,384,1536]{3,2,1,0:T(8,128)(2,1)S(1)} %get-tuple-element.28.oper_ref, f32[2,384,256]{2,1,0:T(8,128)S(1)} %get-tuple-element.46.part_first_ref, f32[2,384,256]{2,1,0:T(8,128)S(1)} %get-tuple-element.47.part_second_ref, ...), custom_call_target="tpu_custom_call" | custom-call | flops 603979776 | bytes 2500000 | tf_op jit(solution)/shard_map/pallas_call | solution.py:279
  49.8 2.7 %shard_map.100 = (bf16[2,1536,128]{2,1,0:T(8,128)(2,1)}, bf16[1536,256]{1,0:T(8,128)(2,1)S(1)}, bf16[1024,256]{1,0:T(8,128)(2,1)S(1)}) custom-call(bf16[4,2,384,1536]{3,2,1,0:T(8,128)(2,1)S(1)} %get-tuple-element.28.oper_ref, f32[2,384,256]{2,1,0:T(8,128)S(1)} %get-tuple-element.49.part_first_ref, f32[2,384,256]{2,1,0:T(8,128)S(1)} %get-tuple-element.50.part_second_ref, ...), custom_call_target="tpu_custom_call" | custom-call | flops 2013265920 | bytes 2000000 | tf_op jit(solution)/shard_map/pallas_call | solution.py:279
  52.6 1.7 %shard_map.101 = bf16[1024,256]{1,0:T(8,128)(2,1)S(1)} custom-call(bf16[8,256,384]{2,1,0:T(8,128)(2,1)S(1)} %copy-done, f32[8,8,256]{2,1,0:T(8,128)S(1)} %shard_map.99.rest_5_.phases_ref, bf16[1536,256]{1,0:T(8,128)(2,1)S(1)} %get-tuple-element.52.vec_ref), custom_call_target="tpu_custom_call" | custom-call | flops 805306368 | bytes 1000000 | tf_op jit(solution)/shard_map/pallas_call | solution.py:279
  54.3 0.2 collective-permute-done.12
  54.7 18.9 %all_to_all.18 = bf16[16,64,256]{2,1,0:T(8,128)(2,1)S(1)} all-to-all(bf16[16,64,256]{2,1,0:T(8,128)(2,1)S(1)} %bitcast.12), channel_id=1, replica_groups={{0,8,32,40,64,72,96,104,128,136,160,168,192,200,224,232},{1,9,33,41,65,..., dimensions={0} | all-to-all | bytes 1048576 | tf_op jit(solution)/shard_map/all_to_all | solution.py:454
  73.6 13.7 %all_to_all.19 = bf16[8,8,256]{2,1,0:T(8,128)(2,1)S(1)} all-to-all(bf16[8,8,256]{2,1,0:T(8,128)(2,1)S(1)} %bitcast.14), channel_id=1, replica_groups={{0,1,2,3,4,5,6,7},{8,9,10,11,12,13,14,15},{16,17,18,19,20,21,22,23},{24..., dimensions={0} | all-to-all | bytes 65536 | tf_op jit(solution)/shard_map/all_to_all | solution.py:456
  87.3 0.6 copy.9
  (24 shorter events, 0.6 us)
Async XLA Ops:
  5.8 11.7 %collective-permute-start = (bf16[384,256]{1,0:T(8,128)(2,1)S(1)}, bf16[384,256]{1,0:T(8,128)(2,1)S(1)}, u32[]{:S(2)}, u32[]{:S(2)}) collective-permute-start(bf16[384,256]{1,0:T(8,128)(2,1)S(1)} %get-tuple-element.33), channel_id=1, source_target_pairs={{0,1},{1,0},{2,3},{3,2},{4,5},{5,4},{6,7},{7,6},{8,9},{9,8},{10,11... | collective-permute-start | bytes 589832 | tf_op jit(solution)/shard_map/ppermute | solution.py:302
  8.6 8.9 %collective-permute-start.1 = (bf16[384,256]{1,0:T(8,128)(2,1)S(1)}, bf16[384,256]{1,0:T(8,128)(2,1)S(1)}, u32[]{:S(2)}, u32[]{:S(2)}) collective-permute-start(bf16[384,256]{1,0:T(8,128)(2,1)S(1)} %get-tuple-element.34), channel_id=1, source_target_pairs={{0,16},{16,0},{32,48},{48,32},{64,80},{80,64},{96,112},{112,96},{1... | collective-permute-start | bytes 589832 | tf_op jit(solution)/shard_map/ppermute | solution.py:302
  8.7 13.1 %collective-permute-start.2 = (bf16[384,256]{1,0:T(8,128)(2,1)S(1)}, bf16[384,256]{1,0:T(8,128)(2,1)S(1)}, u32[]{:S(2)}, u32[]{:S(2)}) collective-permute-start(bf16[384,256]{1,0:T(8,128)(2,1)S(1)} %get-tuple-element.36), channel_id=1, source_target_pairs={{0,15},{1,2},{2,1},{3,4},{4,3},{5,6},{6,5},{7,8},{8,7},{9,10},{10,... | collective-permute-start | bytes 589832 | tf_op jit(solution)/shard_map/ppermute | solution.py:302
  17.1 5.2 %collective-permute-start.3 = (bf16[384,256]{1,0:T(8,128)(2,1)S(1)}, bf16[384,256]{1,0:T(8,128)(2,1)S(1)}, u32[]{:S(2)}, u32[]{:S(2)}) collective-permute-start(bf16[384,256]{1,0:T(8,128)(2,1)S(1)} %get-tuple-element.37), channel_id=1, source_target_pairs={{0,240},{16,32},{32,16},{48,64},{64,48},{80,96},{96,80},{112,128},... | collective-permute-start | bytes 589832 | tf_op jit(solution)/shard_map/ppermute | solution.py:302
  23.6 7.5 %collective-permute-start.5 = (bf16[384,256]{1,0:T(8,128)(2,1)S(1)}, bf16[384,256]{1,0:T(8,128)(2,1)S(1)}, u32[]{:S(2)}, u32[]{:S(2)}) collective-permute-start(bf16[384,256]{1,0:T(8,128)(2,1)S(1)} %shard_map.91), channel_id=1, source_target_pairs={{0,16},{16,0},{32,48},{48,32},{64,80},{80,64},{96,112},{112,96},{1... | collective-permute-start | bytes 589832 | tf_op jit(solution)/shard_map/ppermute | solution.py:302
  23.8 7.3 %collective-permute-start.4 = (bf16[384,256]{1,0:T(8,128)(2,1)S(1)}, bf16[384,256]{1,0:T(8,128)(2,1)S(1)}, u32[]{:S(2)}, u32[]{:S(2)}) collective-permute-start(bf16[384,256]{1,0:T(8,128)(2,1)S(1)} %get-tuple-element.38), channel_id=1, source_target_pairs={{0,1},{1,0},{2,3},{3,2},{4,5},{5,4},{6,7},{7,6},{8,9},{9,8},{10,11... | collective-permute-start | bytes 589832 | tf_op jit(solution)/shard_map/ppermute | solution.py:302
  24.3 8.2 %collective-permute-start.7 = (bf16[384,256]{1,0:T(8,128)(2,1)S(1)}, bf16[384,256]{1,0:T(8,128)(2,1)S(1)}, u32[]{:S(2)}, u32[]{:S(2)}) collective-permute-start(bf16[384,256]{1,0:T(8,128)(2,1)S(1)} %shard_map.93), channel_id=1, source_target_pairs={{0,240},{16,32},{32,16},{48,64},{64,48},{80,96},{96,80},{112,128},... | collective-permute-start | bytes 589832 | tf_op jit(solution)/shard_map/ppermute | solution.py:302
  27.0 9.4 %collective-permute-start.6 = (bf16[384,256]{1,0:T(8,128)(2,1)S(1)}, bf16[384,256]{1,0:T(8,128)(2,1)S(1)}, u32[]{:S(2)}, u32[]{:S(2)}) collective-permute-start(bf16[384,256]{1,0:T(8,128)(2,1)S(1)} %get-tuple-element.42), channel_id=1, source_target_pairs={{0,15},{1,2},{2,1},{3,4},{4,3},{5,6},{6,5},{7,8},{8,7},{9,10},{10,... | collective-permute-start | bytes 589832 | tf_op jit(solution)/shard_map/ppermute | solution.py:302
  37.2 9.2 %copy-start.1 = (f32[8,2,256]{2,1,0:T(2,128)S(1)}, f32[8,2,256]{2,1,0:T(2,128)}, u32[]{:S(2)}) copy-start(f32[8,2,256]{2,1,0:T(2,128)} %constant.8.clone.cosines_ref) | copy-start | bytes 49156
  37.2 9.2 %copy-start.2 = (s32[1,1,2]{2,1,0:T(1,128)S(1)}, s32[1,1,2]{2,1,0:T(1,128)}, u32[]{:S(2)}) copy-start(s32[1,1,2]{2,1,0:T(1,128)} %param.11) | copy-start | bytes 28
  37.7 9.7 %collective-permute-start.9 = (bf16[384,256]{1,0:T(8,128)(2,1)S(1)}, bf16[384,256]{1,0:T(8,128)(2,1)S(1)}, u32[]{:S(2)}, u32[]{:S(2)}) collective-permute-start(bf16[384,256]{1,0:T(8,128)(2,1)S(1)} %shard_map.95), channel_id=1, source_target_pairs={{0,16},{16,0},{32,48},{48,32},{64,80},{80,64},{96,112},{112,96},{1... | collective-permute-start | bytes 589832 | tf_op jit(solution)/shard_map/ppermute | solution.py:302
  37.8 9.6 %collective-permute-start.8 = (bf16[384,256]{1,0:T(8,128)(2,1)S(1)}, bf16[384,256]{1,0:T(8,128)(2,1)S(1)}, u32[]{:S(2)}, u32[]{:S(2)}) collective-permute-start(bf16[384,256]{1,0:T(8,128)(2,1)S(1)} %get-tuple-element.43), channel_id=1, source_target_pairs={{0,1},{1,0},{2,3},{3,2},{4,5},{5,4},{6,7},{7,6},{8,9},{9,8},{10,11... | collective-permute-start | bytes 589832 | tf_op jit(solution)/shard_map/ppermute | solution.py:302
  38.1 10.7 %collective-permute-start.10 = (bf16[384,256]{1,0:T(8,128)(2,1)S(1)}, bf16[384,256]{1,0:T(8,128)(2,1)S(1)}, u32[]{:S(2)}, u32[]{:S(2)}) collective-permute-start(bf16[384,256]{1,0:T(8,128)(2,1)S(1)} %get-tuple-element.48), channel_id=1, source_target_pairs={{0,15},{1,2},{2,1},{3,4},{4,3},{5,6},{6,5},{7,8},{8,7},{9,10},{10,... | collective-permute-start | bytes 589832 | tf_op jit(solution)/shard_map/ppermute | solution.py:302
  43.5 6.3 %collective-permute-start.11 = (bf16[384,256]{1,0:T(8,128)(2,1)S(1)}, bf16[384,256]{1,0:T(8,128)(2,1)S(1)}, u32[]{:S(2)}, u32[]{:S(2)}) collective-permute-start(bf16[384,256]{1,0:T(8,128)(2,1)S(1)} %shard_map.98), channel_id=1, source_target_pairs={{0,240},{16,32},{32,16},{48,64},{64,48},{80,96},{96,80},{112,128},... | collective-permute-start | bytes 589832 | tf_op jit(solution)/shard_map/ppermute | solution.py:302
  47.4 2.4 %copy-start = (bf16[8,256,384]{2,1,0:T(8,128)(2,1)S(1)}, bf16[8,256,384]{2,1,0:T(8,128)(2,1)}, u32[]{:S(2)}) copy-start(bf16[8,256,384]{2,1,0:T(8,128)(2,1)} %constant.9.clone.rest_4_.tables_ref) | copy-start | bytes 4718596
  52.5 2.0 %collective-permute-start.12 = (bf16[1024,256]{1,0:T(8,128)(2,1)S(1)}, bf16[1024,256]{1,0:T(8,128)(2,1)S(1)}, u32[]{:S(2)}, u32[]{:S(2)}) collective-permute-start(bf16[1024,256]{1,0:T(8,128)(2,1)S(1)} %get-tuple-element.53), channel_id=1, source_target_pairs={{0,16},{16,0},{32,48},{48,32},{64,80},{80,64},{96,112},{112,96},{1... | collective-permute-start | bytes 1572872 | tf_op jit(solution)/shard_map/ppermute | solution.py:442
